TPU v7x, 32 devices: a whole 2x2x4 slice. The times are simulated.
32 devices in a mesh: row: 8 (over z, y), col: 4 (over x, core).
Axes of the slice: x: 2, y: 2, z: 4, core: 2. Of those that a mesh axis runs over, the one named last changes fastest.
Arguments:
- obs_panel: bfloat16 [196608, 2048], P('row', 'col'), may hold values from -0.1875 to 0.1875
- skies: bfloat16 [196608, 256], P('row', 'col'), may hold values from -6 to 6
- panel_index: int32 [2048], replicated, may hold values from 0 to 196607
- prior_sum: float32 [196608, 256], P('row', 'col'), may hold values from -6 to 6
- apod: float32 [196608], P('row'), may hold values from 0.05 to 1
- proj_panel: bfloat16 [2048, 196608], P(None, ('row', 'col')), may hold values from -0.02734375 to 0.02734375
Outputs:
- reobserved: float32 [196608, 256], P('row', 'col')
- projection: float32 [2048, 256], P('row', 'col')
Inputs may be any that keep to these rules, and one draw needn't show every extreme that they name: `panel_index`: rows of the observed patch; a row may appear more than once.
All inputs are finite; a program needn't handle non-finite values.
Results may differ from a plain program's by a relative error of at most 0.0029.
Values may be sent and summed in bfloat16 or wider, within the bound.
A program may use at most 192 MiB of HBM per device.

v0:
```python
import functools
import math

import jax
import jax.numpy as jnp
from jax import lax
from jax.experimental import pallas as pl
from jax.experimental.pallas import tpu as pltpu
from jax.sharding import PartitionSpec as P

MESH = pl.DeviceIdType.MESH
NT = (((1,), (1,)), ((), ()))
UNIT = 256
D2, D3, D4 = 1, 3, 5
LIMIT = 48 * 1024 * 1024


def remote(src, dst, send, recv, row, col):
    return pltpu.make_async_remote_copy(
        src_ref=src, dst_ref=dst, send_sem=send, recv_sem=recv, device_id=(row, col), device_id_type=MESH
    )


def spread_kernel(n_row, n_col, own_ref, out_ref, land, mine, gather, send1, recv1, send2, recv2):
    r, c = lax.axis_index("row"), lax.axis_index("col")
    sims, panel = own_ref.shape
    part = panel // n_row
    rep = n_row // n_col
    first = []
    for d in range(1, n_row):
        to = lax.rem(r + d, n_row)
        cp = remote(own_ref.at[:, pl.ds(pl.multiple_of(to * part, part), part)], land.at[d - 1],
                    send1.at[d - 1], recv1.at[d - 1], to, c)
        cp.start()
        first.append(cp)
    total = own_ref[:, pl.ds(pl.multiple_of(r * part, part), part)].astype(jnp.float32)
    for d in range(1, n_row):
        first[d - 1].wait_recv()
        total = total + land[d - 1].astype(jnp.float32)
    mine[...] = total.astype(mine.dtype)
    sub = lax.rem(r, rep)
    col_to = lax.div(r, rep)
    slot = sub * n_col + c
    second = []
    for d in range(n_row):
        to = lax.rem(r + d, n_row)
        cp = remote(mine, gather.at[slot], send2.at[d], recv2.at[slot], to, col_to)
        second.append(cp)
        if d > 0:
            cp.start()
        else:
            @pl.when(col_to != c)
            def _():
                cp.start()

            @pl.when(col_to == c)
            def _():
                gather[slot] = mine[...]
    for s in range(rep):
        for j in range(n_col):
            here = (c * rep + s == r) & (c == j)

            @pl.when(jnp.logical_not(here))
            def _():
                remote(mine, gather.at[s * n_col + j], send2.at[0], recv2.at[s * n_col + j], r, c).wait_recv()
    chips = n_col // 2
    core, chip = lax.rem(c, 2), lax.div(c, 2)
    for q in range(n_col):
        other, shift = q // chips, q % chips
        source = lax.rem(chip + shift, chips) * 2 + (core if other == 0 else 1 - core)
        for s in range(rep):
            out_ref[q * sims:(q + 1) * sims, s * part:(s + 1) * part] = gather[s * n_col + source]
    for cp in first:
        cp.wait_send()
    for d in range(n_row):
        if d > 0:
            second[d].wait_send()
        else:
            @pl.when(col_to != c)
            def _():
                second[0].wait_send()


def spread(own, n_row, n_col):
    sims, panel = own.shape
    part = panel // n_row
    vmem = pl.BlockSpec(memory_space=pltpu.VMEM)
    return pl.pallas_call(
        functools.partial(spread_kernel, n_row, n_col),
        out_shape=jax.ShapeDtypeStruct((sims * n_col, panel // n_col), own.dtype),
        in_specs=[vmem],
        out_specs=vmem,
        scratch_shapes=[
            pltpu.VMEM((n_row - 1, sims, part), own.dtype),
            pltpu.VMEM((sims, part), own.dtype),
            pltpu.VMEM((n_row, sims, part), own.dtype),
            pltpu.SemaphoreType.DMA((n_row - 1,)),
            pltpu.SemaphoreType.DMA((n_row - 1,)),
            pltpu.SemaphoreType.DMA((n_row,)),
            pltpu.SemaphoreType.DMA((n_row,)),
        ],
        compiler_params=pltpu.CompilerParams(has_side_effects=True, vmem_limit_bytes=LIMIT),
        name="spread",
    )(own)


def fold_kernel(n_row, n_col, acc_ref, out_ref, land_a, sum_a, land_b, sum_b, land_c, sa, ra, sb, rb, sc, rc):
    r, c = lax.axis_index("row"), lax.axis_index("col")
    chips = n_col // 2
    core, chip = lax.rem(c, 2), lax.div(c, 2)
    out_rows = out_ref.shape[1]

    def block(col):
        return lax.rem(c - col + n_col, n_col)

    a = []
    for b in range(chips):
        to = lax.rem(chip + b, chips)
        cp = remote(acc_ref.at[block(to * 2 + 1 - core)], land_a.at[b], sa.at[b], ra.at[b], r, chip * 2 + 1 - core)
        cp.start()
        a.append(cp)
    bs = []
    for s in list(range(1, chips)) + [0]:
        to = lax.rem(chip + s, chips)
        a[s].wait_recv()
        sum_a[s] = acc_ref[block(to * 2 + core)] + land_a[s]
        if s > 0:
            cp = remote(sum_a.at[s], land_b.at[s - 1], sb.at[s - 1], rb.at[s - 1], r, to * 2 + core)
            cp.start()
            bs.append(cp)
    total = sum_a[0]
    for s in range(1, chips):
        bs[s - 1].wait_recv()
        total = total + land_b[s - 1]
    sum_b[...] = total
    cs = []
    for d in range(1, n_row):
        to = lax.rem(r + d, n_row)
        cp = remote(sum_b.at[:, pl.ds(pl.multiple_of(to * out_rows, out_rows), out_rows)], land_c.at[d - 1],
                    sc.at[d - 1], rc.at[d - 1], to, c)
        cp.start()
        cs.append(cp)
    total = sum_b[:, pl.ds(pl.multiple_of(r * out_rows, out_rows), out_rows)]
    for d in range(1, n_row):
        cs[d - 1].wait_recv()
        total = total + land_c[d - 1]
    out_ref[...] = total
    for cp in a + bs + cs:
        cp.wait_send()


def fold(acc, n_row, n_col):
    _, sims, prows = acc.shape
    chips = n_col // 2
    vmem = pl.BlockSpec(memory_space=pltpu.VMEM)
    dma = pltpu.SemaphoreType.DMA
    return pl.pallas_call(
        functools.partial(fold_kernel, n_row, n_col),
        out_shape=jax.ShapeDtypeStruct((sims, prows // n_row), jnp.float32),
        in_specs=[vmem],
        out_specs=vmem,
        scratch_shapes=[
            pltpu.VMEM((chips, sims, prows), jnp.float32),
            pltpu.VMEM((chips, sims, prows), jnp.float32),
            pltpu.VMEM((chips - 1, sims, prows), jnp.float32),
            pltpu.VMEM((sims, prows), jnp.float32),
            pltpu.VMEM((n_row - 1, sims, prows // n_row), jnp.float32),
            dma((chips,)), dma((chips,)), dma((chips - 1,)), dma((chips - 1,)), dma((n_row - 1,)), dma((n_row - 1,)),
        ],
        compiler_params=pltpu.CompilerParams(has_side_effects=True, vmem_limit_bytes=LIMIT),
        name="fold",
    )(acc)


def stream_kernel(n_col, units, p_ref, o_ref, *refs):
    priors, (apod_ref, proj_ref) = refs[:n_col], refs[n_col:n_col + 2]
    re_ref, acc_ref = refs[n_col + 2:n_col + 4]
    keep, swap, near, fars, far, ws, wr, ss, sr, fs, fr, gs, gr = refs[n_col + 4:]
    r, c = lax.axis_index("row"), lax.axis_index("col")
    chips = n_col // 2
    core, chip = lax.rem(c, 2), lax.div(c, 2)
    sims, size = wr.shape[2:]
    g = pl.program_id(0)

    def near_copy(u):
        k, q = lax.rem(u, swap.shape[0]), lax.rem(u, near.shape[0])
        return remote(swap.at[k], near.at[q], ss.at[k], sr.at[q], r, chip * 2 + 1 - core)

    def far_copies(u):
        k, q = lax.rem(u, fars.shape[0]), lax.rem(u, far.shape[0])
        return [remote(fars.at[k, s], far.at[q, s], fs.at[k, s], fr.at[q, s], r, lax.rem(chip + s + 1, chips) * 2 + core)
                for s in range(chips - 1)]

    def weighted_copies(u):
        k, q = lax.rem(u, ws.shape[0]), lax.rem(u, wr.shape[0])
        return [remote(ws.at[k, d], wr.at[q, d - 1], gs.at[k, d - 1], gr.at[q, d - 1], r, lax.rem(c + d, n_col))
                for d in range(1, n_col)]

    @pl.when(g == 0)
    def _():
        acc_ref[...] = jnp.zeros_like(acc_ref)

    @pl.when((g >= D2) & (g < units + D2))
    def _():
        u = g - D2
        near_copy(u).wait_recv()

        @pl.when(u >= fars.shape[0])
        def _():
            for cp in far_copies(u - fars.shape[0]):
                cp.wait_send()

        k, q, e = lax.rem(u, fars.shape[0]), lax.rem(u, near.shape[0]), lax.rem(u, keep.shape[0])
        copies = far_copies(u)
        for s in range(chips - 1):
            away = slice((s + 1) * sims, (s + 2) * sims)
            fars[k, s] = (keep[e, away] + near[q, away].astype(jnp.float32)).astype(jnp.bfloat16)
            copies[s].start()
        keep[e, :sims] = keep[e, :sims] + near[q, :sims].astype(jnp.float32)

    @pl.when((g >= D3) & (g < units + D3))
    def _():
        u = g - D3
        for cp in far_copies(u):
            cp.wait_recv()

        @pl.when(u >= ws.shape[0])
        def _():
            for cp in weighted_copies(u - ws.shape[0]):
                cp.wait_send()

        k, q, e = lax.rem(u, ws.shape[0]), lax.rem(u, far.shape[0]), lax.rem(u, keep.shape[0])
        for i in range(n_col):
            lanes = slice(i * size, (i + 1) * size)
            total = keep[e, :sims, lanes]
            for s in range(chips - 1):
                total = total + far[q, s, :, lanes].astype(jnp.float32)
            total = priors[i][...] + total
            re_ref[i] = total
            ws[k, lax.rem(i - c + n_col, n_col)] = (apod_ref[i:i + 1, :] * total).astype(jnp.bfloat16)
        for cp in weighted_copies(u):
            cp.start()

    @pl.when(g < units)
    def _():
        k, e = lax.rem(g, swap.shape[0]), lax.rem(g, keep.shape[0])

        @pl.when(g >= swap.shape[0])
        def _():
            near_copy(g - swap.shape[0]).wait_send()

        kept = n_col * sims // 2
        rows = o_ref[...].reshape(n_col * size, o_ref.shape[2])
        value = lax.dot_general(p_ref[...], rows, NT, preferred_element_type=jnp.float32)
        swap[k] = value[kept:].astype(jnp.bfloat16)
        near_copy(g).start()
        keep[e] = value[:kept]

    @pl.when(g >= D4)
    def _():
        u = g - D4
        for cp in weighted_copies(u):
            cp.wait_recv()
        k, q = lax.rem(u, ws.shape[0]), lax.rem(u, wr.shape[0])
        w = jnp.concatenate([ws[k, 0]] + [wr[q, d] for d in range(n_col - 1)], axis=0)
        prows = proj_ref.shape[0]
        tile = min(512, prows)
        for j in range(0, prows, tile):
            value = lax.dot_general(w, proj_ref[j:j + tile, :], NT, preferred_element_type=jnp.float32)
            for d in range(n_col):
                acc_ref[d, :, j:j + tile] += value[d * sims:(d + 1) * sims]

    @pl.when(g == units + D4 - 1)
    def _():
        for b in range(min(units, swap.shape[0])):
            near_copy(units - 1 - b).wait_send()
        for b in range(min(units, fars.shape[0])):
            for cp in far_copies(units - 1 - b):
                cp.wait_send()
        for b in range(min(units, ws.shape[0])):
            for cp in weighted_copies(units - 1 - b):
                cp.wait_send()


def stream(picked, obs, prior, apod, proj, n_col):
    depth, (sims, rows), prows = obs.shape[1], prior.shape, proj.shape[0]
    slab = rows // n_col
    units = slab // math.gcd(slab, UNIT)
    size = slab // units
    kept = n_col * sims // 2
    chips = n_col // 2

    def at(g, lag):
        return jnp.clip(g - lag, 0, units - 1)

    n_near, n_far, n_got = 2 * D2, 2 * D3 + 2 - 2 * D2, 2 * D4 + 2 - 2 * D3
    n_ws = D4 - D3 + 2
    wide = n_col * size
    dma, bf16 = pltpu.SemaphoreType.DMA, jnp.bfloat16
    prior_specs = [pl.BlockSpec((sims, size), functools.partial(lambda g, i: (0, i * units + at(g, D3)), i=i)) for i in range(n_col)]
    return pl.pallas_call(
        functools.partial(stream_kernel, n_col, units),
        grid=(units + D4,),
        in_specs=[
            pl.BlockSpec(picked.shape, lambda g: (0, 0)),
            pl.BlockSpec((n_col, size, depth), lambda g: (0, at(g, 0), 0)),
            *prior_specs,
            pl.BlockSpec((n_col, size), lambda g: (0, at(g, D3))),
            pl.BlockSpec((prows, size), lambda g: (0, at(g, D4))),
        ],
        out_specs=[
            pl.BlockSpec((n_col, sims, size), lambda g: (0, 0, at(g, D3))),
            pl.BlockSpec((n_col, sims, prows), lambda g: (0, 0, 0)),
        ],
        out_shape=[
            jax.ShapeDtypeStruct((n_col, sims, slab), jnp.float32),
            jax.ShapeDtypeStruct((n_col, sims, prows), jnp.float32),
        ],
        scratch_shapes=[
            pltpu.VMEM((D3 + 1, kept, wide), jnp.float32),
            pltpu.VMEM((2, kept, wide), bf16),
            pltpu.VMEM((n_near, kept, wide), bf16),
            pltpu.VMEM((2, chips - 1, sims, wide), bf16),
            pltpu.VMEM((n_far, chips - 1, sims, wide), bf16),
            pltpu.VMEM((n_ws, n_col, sims, size), bf16),
            pltpu.VMEM((n_got, n_col - 1, sims, size), bf16),
            dma((2,)), dma((n_near,)), dma((2, chips - 1)), dma((n_far, chips - 1)),
            dma((n_ws, n_col - 1)), dma((n_got, n_col - 1)),
        ],
        compiler_params=pltpu.CompilerParams(has_side_effects=True, vmem_limit_bytes=LIMIT, dimension_semantics=("arbitrary",)),
        name="stream",
    )(picked, obs.reshape(n_col, slab, depth), *[prior] * n_col, apod.reshape(n_col, slab), proj)


def on_device(n_row, n_col, obs_panel, skies, panel_index, prior_sum, apod, proj_panel):
    rows_blk, sims = skies.shape
    local_idx = panel_index - lax.axis_index("row") * rows_blk
    inside = (local_idx >= 0) & (local_idx < rows_blk)
    taken = jnp.take(skies, jnp.clip(local_idx, 0, rows_blk - 1), axis=0)
    own = jnp.where(inside[:, None], taken, jnp.zeros((), jnp.bfloat16)).T
    picked = spread(own, n_row, n_col)

    out, acc = stream(picked, obs_panel, prior_sum.T, apod, proj_panel, n_col)
    projection = fold(acc, n_row, n_col)
    return out.transpose(0, 2, 1).reshape(rows_blk, sims), projection.T


def solution(mesh):
    in_specs = (P("row", "col"), P("row", "col"), P(), P("row", "col"), P("row"), P(None, ("row", "col")))
    out_specs = (P("row", "col"), P("row", "col"))
    body = functools.partial(on_device, mesh.shape["row"], mesh.shape["col"])
    return jax.shard_map(body, mesh=mesh, in_specs=in_specs, out_specs=out_specs, check_vma=False)
```

profile of v0, /device:TPU:0, one launch (start us, length us, event | category | flops | bytes accessed | tf_op | source)
XLA Modules:
  0.0 194.0 jit_solution(9021006906549397285)
XLA Ops:
  0.6 0.7 compare_and_fusion.1
  1.3 0.7 fusion
  2.1 0.9 reshape.20.refs_4_
  3.0 6.6 %copy.10 = bf16[24576,64]{1,0:T(8,128)(2,1)} copy(bf16[24576,64]{0,1:T(8,128)(2,1)} %param.7) | data formatting | bytes 6291456 | tf_op args[1]
  9.5 9.2 %gather_fusion = bf16[2048,64]{1,0:T(8,128)(2,1)S(1)} fusion(bf16[24576,64]{1,0:T(8,128)(2,1)} %copy.10, s32[2048]{0:T(1024)S(1)} %fusion), kind=kCustom, calls=%fused_computation | custom fusion | bytes 532480 | tf_op jit(solution)/shard_map/jit(_take)/gather | solution.py:339
  18.7 0.2 copy.11
  19.0 21.0 %spread.1.p_ref = bf16[256,512]{1,0:T(8,128)(2,1)S(1)} custom-call(bf16[64,2048]{1,0:T(8,128)(2,1)S(1)} %select_bitcast_fusion.own_ref), custom_call_target="tpu_custom_call" | custom-call | tf_op jit(solution)/shard_map/spread/pallas_call | solution.py:88
  40.0 113.8 %stream.1 = (f32[4,64,6144]{2,1,0:T(8,128)}, f32[4,64,2048]{2,1,0:T(8,128)S(1)}) custom-call(bf16[256,512]{1,0:T(8,128)(2,1)S(1)} %spread.1.p_ref, bf16[4,6144,512]{2,1,0:T(8,128)(2,1)} %bitcast.13, f32[64,24576]{1,0:T(8,128)} %bitcast.9, f32[64,24576]{1,0:T(8,128)} %bitcast.10, f32[64,24576]{1,0:T(8,128)} %bitcast.11, f32[64,24576]{1,0:T(8,128)} %bitcast.12, ...), custom_call_target="tpu_custom_call" | custom-call | tf_op jit(solution)/shard_map/stream/pallas_call | solution.py:301
  153.9 6.2 %copy.13 = f32[4,8,8,6144]{3,2,0,1:T(8,128)} copy(f32[4,8,8,6144]{3,2,1,0:T(8,128)} %bitcast.15) | data formatting | bytes 12582912 | tf_op jit(solution)/shard_map/reshape | solution.py:345
  160.1 33.3 %fold.1 = f32[64,256]{1,0:T(8,128)S(1)} custom-call(f32[4,64,2048]{2,1,0:T(8,128)S(1)} %get-tuple-element.5.acc_ref), custom_call_target="tpu_custom_call" | custom-call | tf_op jit(solution)/shard_map/fold/pallas_call | solution.py:157
  193.4 0.6 copy.15
  (1 shorter events, 0.0 us)
where the time goes:
time: 195 us; the launch traced here: 194 us
  Pallas kernels  168 us (86%)
  local copies, waits for them, and re-layouts  23.7 us (12%)
    pallas_call x1, Pallas kernels, stream(): pl.pallas_call(functools.partial(stream_kernel, n_col, units), grid=(unit...  114 us
    pallas_call x1, Pallas kernels, fold(): pl.pallas_call(functools.partial(fold_kernel, n_row, n_col), out_shape=ja...  33.3 us
    pallas_call x1, Pallas kernels, spread(): pl.pallas_call(functools.partial(spread_kernel, n_row, n_col), out_shape=...  21 us
    gather x2, local copies, waits for them, and re-layouts, on_device(): taken = jnp.take(skies, jnp.clip(local_idx, 0, rows_blk - 1), axis=0)  9.38 us
    unnamed x2, local copies, waits for them, and re-layouts  7.18 us
    reshape x1, local copies, waits for them, and re-layouts, on_device(): return (out.transpose(0, 2, 1).reshape(rows_blk, sims), projection.T)  6.17 us

commit v1 on v0

--- a/solution.py
+++ b/solution.py
@@ -26,20 +26,24 @@
     sims, panel = own_ref.shape
     part = panel // n_row
     rep = n_row // n_col
+
+    def part_of(row):
+        return lax.rem(row, 2) * (n_row // 2) + lax.div(row, 2)
+
     first = []
     for d in range(1, n_row):
         to = lax.rem(r + d, n_row)
-        cp = remote(own_ref.at[:, pl.ds(pl.multiple_of(to * part, part), part)], land.at[d - 1],
+        cp = remote(own_ref.at[:, pl.ds(pl.multiple_of(part_of(to) * part, part), part)], land.at[d - 1],
                     send1.at[d - 1], recv1.at[d - 1], to, c)
         cp.start()
         first.append(cp)
-    total = own_ref[:, pl.ds(pl.multiple_of(r * part, part), part)].astype(jnp.float32)
+    total = own_ref[:, pl.ds(pl.multiple_of(part_of(r) * part, part), part)].astype(jnp.float32)
     for d in range(1, n_row):
         first[d - 1].wait_recv()
         total = total + land[d - 1].astype(jnp.float32)
     mine[...] = total.astype(mine.dtype)
-    sub = lax.rem(r, rep)
-    col_to = lax.div(r, rep)
+    sub = lax.rem(part_of(r), rep)
+    col_to = lax.div(part_of(r), rep)
     slot = sub * n_col + c
     second = []
     for d in range(n_row):
@@ -58,7 +62,7 @@
                 gather[slot] = mine[...]
     for s in range(rep):
         for j in range(n_col):
-            here = (c * rep + s == r) & (c == j)
+            here = (c * rep + s == part_of(r)) & (c == j)
 
             @pl.when(jnp.logical_not(here))
             def _():
@@ -104,78 +108,107 @@
     )(own)
 
 
-def fold_kernel(n_row, n_col, acc_ref, out_ref, land_a, sum_a, land_b, sum_b, land_c, sa, ra, sb, rb, sc, rc):
+def fold_kernel(n_row, n_col, acc_ref, swapped_ref, out_ref, sa, lx0, b0, ly0, ly1, b1, lx1, ends, lz,
+                sx0, rx0, sy, ry, sx1, rx1, sz, rz):
     r, c = lax.axis_index("row"), lax.axis_index("col")
-    chips = n_col // 2
+    chips, pairs = n_col // 2, n_row // 2
     core, chip = lax.rem(c, 2), lax.div(c, 2)
-    out_rows = out_ref.shape[1]
-
-    def block(col):
-        return lax.rem(c - col + n_col, n_col)
-
-    a = []
-    for b in range(chips):
-        to = lax.rem(chip + b, chips)
-        cp = remote(acc_ref.at[block(to * 2 + 1 - core)], land_a.at[b], sa.at[b], ra.at[b], r, chip * 2 + 1 - core)
+    low, high = lax.rem(r, 2), lax.div(r, 2)
+    beside = high * 2 + 1 - low
+    sims, pb = out_ref.shape
+    hs, half = sims // 2, pairs * pb
+
+    def side(which):
+        return pl.ds(pl.multiple_of(which * half, half), half)
+
+    def to_col(s):
+        return lax.rem(chip + s, chips) * 2 + core
+
+    copies = []
+
+    def go(*args):
+        cp = remote(*args)
         cp.start()
-        a.append(cp)
-    bs = []
-    for s in list(range(1, chips)) + [0]:
-        to = lax.rem(chip + s, chips)
-        a[s].wait_recv()
-        sum_a[s] = acc_ref[block(to * 2 + core)] + land_a[s]
+        copies.append(cp)
+        return cp
+
+    order = list(range(1, chips)) + [0]
+    x0 = []
+    for s in order:
+        mine = (chips - s) % chips
+        theirs = lax.rem(2 * chips - s - core, chips)
+        for k in range(n_row):
+            from_lanes = slice(k * pb, (k + 1) * pb)
+            at = (k % 2) * half + (k // 2) * pb
+            for h in range(2):
+                rows = slice(h * hs, (h + 1) * hs)
+                sa[h, s, :, at:at + pb] = acc_ref[mine, rows, from_lanes] + swapped_ref[theirs, rows, from_lanes]
         if s > 0:
-            cp = remote(sum_a.at[s], land_b.at[s - 1], sb.at[s - 1], rb.at[s - 1], r, to * 2 + core)
-            cp.start()
-            bs.append(cp)
-    total = sum_a[0]
+            x0.append(go(sa.at[0, s], lx0.at[s - 1], sx0.at[s - 1], rx0.at[s - 1], r, to_col(s)))
+    y1 = go(sa.at[1, :, :, side(1 - low)], ly1, sy.at[1], ry.at[1], beside, c)
+    total = sa[0, 0]
     for s in range(1, chips):
-        bs[s - 1].wait_recv()
-        total = total + land_b[s - 1]
-    sum_b[...] = total
-    cs = []
-    for d in range(1, n_row):
-        to = lax.rem(r + d, n_row)
-        cp = remote(sum_b.at[:, pl.ds(pl.multiple_of(to * out_rows, out_rows), out_rows)], land_c.at[d - 1],
-                    sc.at[d - 1], rc.at[d - 1], to, c)
-        cp.start()
-        cs.append(cp)
-    total = sum_b[:, pl.ds(pl.multiple_of(r * out_rows, out_rows), out_rows)]
-    for d in range(1, n_row):
-        cs[d - 1].wait_recv()
-        total = total + land_c[d - 1]
-    out_ref[...] = total
-    for cp in a + bs + cs:
+        x0[s - 1].wait_recv()
+        total = total + lx0[s - 1]
+    b0[...] = total
+    y0 = go(b0.at[:, side(1 - low)], ly0, sy.at[0], ry.at[0], beside, c)
+    y1.wait_recv()
+    b1[...] = sa[1, :, :, side(low)] + ly1[...]
+    x1 = [go(b1.at[s], lx1.at[s - 1], sx1.at[s - 1], rx1.at[s - 1], r, to_col(s)) for s in range(1, chips)]
+    z = []
+    for h in range(2):
+        if h == 0:
+            y0.wait_recv()
+            ends[0] = b0[:, side(low)] + ly0[...]
+        else:
+            total = b1[0]
+            for s in range(1, chips):
+                x1[s - 1].wait_recv()
+                total = total + lx1[s - 1]
+            ends[1] = total
+        for d in range(1, pairs):
+            to = lax.rem(high + d, pairs)
+            z.append(go(ends.at[h, :, pl.ds(pl.multiple_of(to * pb, pb), pb)], lz.at[h, d - 1], sz.at[h, d - 1], rz.at[h, d - 1], to * 2 + low, c))
+    for h in range(2):
+        total = ends[h, :, pl.ds(pl.multiple_of(high * pb, pb), pb)]
+        for d in range(1, pairs):
+            z[h * (pairs - 1) + d - 1].wait_recv()
+            total = total + lz[h, d - 1]
+        out_ref[h * hs:(h + 1) * hs, :] = total
+    for cp in copies:
         cp.wait_send()
 
 
-def fold(acc, n_row, n_col):
+def fold(acc, swapped, n_row, n_col):
     _, sims, prows = acc.shape
-    chips = n_col // 2
+    chips, pairs = n_col // 2, n_row // 2
+    hs, pb, half = sims // 2, prows // n_row, prows // 2
     vmem = pl.BlockSpec(memory_space=pltpu.VMEM)
     dma = pltpu.SemaphoreType.DMA
+
+    def f32(*shape):
+        return pltpu.VMEM(shape, jnp.float32)
+
     return pl.pallas_call(
         functools.partial(fold_kernel, n_row, n_col),
-        out_shape=jax.ShapeDtypeStruct((sims, prows // n_row), jnp.float32),
-        in_specs=[vmem],
+        out_shape=jax.ShapeDtypeStruct((sims, pb), jnp.float32),
+        in_specs=[vmem] * 2,
         out_specs=vmem,
         scratch_shapes=[
-            pltpu.VMEM((chips, sims, prows), jnp.float32),
-            pltpu.VMEM((chips, sims, prows), jnp.float32),
-            pltpu.VMEM((chips - 1, sims, prows), jnp.float32),
-            pltpu.VMEM((sims, prows), jnp.float32),
-            pltpu.VMEM((n_row - 1, sims, prows // n_row), jnp.float32),
-            dma((chips,)), dma((chips,)), dma((chips - 1,)), dma((chips - 1,)), dma((n_row - 1,)), dma((n_row - 1,)),
+            f32(2, chips, hs, prows), f32(chips - 1, hs, prows), f32(hs, prows), f32(hs, half),
+            f32(chips, hs, half), f32(chips, hs, half), f32(chips - 1, hs, half), f32(2, hs, half), f32(2, pairs - 1, hs, pb),
+            dma((chips - 1,)), dma((chips - 1,)), dma((2,)), dma((2,)),
+            dma((chips - 1,)), dma((chips - 1,)), dma((2, pairs - 1)), dma((2, pairs - 1)),
         ],
         compiler_params=pltpu.CompilerParams(has_side_effects=True, vmem_limit_bytes=LIMIT),
         name="fold",
-    )(acc)
+    )(acc, swapped)
 
 
 def stream_kernel(n_col, units, p_ref, o_ref, *refs):
     priors, (apod_ref, proj_ref) = refs[:n_col], refs[n_col:n_col + 2]
-    re_ref, acc_ref = refs[n_col + 2:n_col + 4]
-    keep, swap, near, fars, far, ws, wr, ss, sr, fs, fr, gs, gr = refs[n_col + 4:]
+    re_ref, *accs = refs[n_col + 2:n_col + 5]
+    keep, swap, near, fars, far, ws, wr, ss, sr, fs, fr, gs, gr = refs[n_col + 5:]
     r, c = lax.axis_index("row"), lax.axis_index("col")
     chips = n_col // 2
     core, chip = lax.rem(c, 2), lax.div(c, 2)
@@ -198,7 +231,8 @@
 
     @pl.when(g == 0)
     def _():
-        acc_ref[...] = jnp.zeros_like(acc_ref)
+        for acc in accs:
+            acc[...] = jnp.zeros_like(acc)
 
     @pl.when((g >= D2) & (g < units + D2))
     def _():
@@ -268,7 +302,7 @@
         for j in range(0, prows, tile):
             value = lax.dot_general(w, proj_ref[j:j + tile, :], NT, preferred_element_type=jnp.float32)
             for d in range(n_col):
-                acc_ref[d, :, j:j + tile] += value[d * sims:(d + 1) * sims]
+                accs[d % 2][d // 2, :, j:j + tile] += value[d * sims:(d + 1) * sims]
 
     @pl.when(g == units + D4 - 1)
     def _():
@@ -310,11 +344,11 @@
         ],
         out_specs=[
             pl.BlockSpec((n_col, sims, size), lambda g: (0, 0, at(g, D3))),
-            pl.BlockSpec((n_col, sims, prows), lambda g: (0, 0, 0)),
+            *[pl.BlockSpec((chips, sims, prows), lambda g: (0, 0, 0))] * 2,
         ],
         out_shape=[
             jax.ShapeDtypeStruct((n_col, sims, slab), jnp.float32),
-            jax.ShapeDtypeStruct((n_col, sims, prows), jnp.float32),
+            *[jax.ShapeDtypeStruct((chips, sims, prows), jnp.float32)] * 2,
         ],
         scratch_shapes=[
             pltpu.VMEM((D3 + 1, kept, wide), jnp.float32),
@@ -340,8 +374,9 @@
     own = jnp.where(inside[:, None], taken, jnp.zeros((), jnp.bfloat16)).T
     picked = spread(own, n_row, n_col)
 
-    out, acc = stream(picked, obs_panel, prior_sum.T, apod, proj_panel, n_col)
-    projection = fold(acc, n_row, n_col)
+    out, acc, other = stream(picked, obs_panel, prior_sum.T, apod, proj_panel, n_col)
+    swapped = lax.ppermute(other, "col", [(i, i ^ 1) for i in range(n_col)])
+    projection = fold(acc, swapped, n_row, n_col)
     return out.transpose(0, 2, 1).reshape(rows_blk, sims), projection.T
 
 

time: 195 us -> 186 us (0.954)
  Pallas kernels: 168 us -> 161 us
    pallas_call x1, Pallas kernels: 33.3 us -> 25.3 us  [fold(): pl.pallas_call(functools.partial(fold_kernel, n_row, n_col), out_shape=ja...]
    unnamed x2 -> x4, local copies, waits for them, and re-layouts: 7.18 us -> 7.22 us
  transfers between devices with their start and end apart: 0 -> 1, of which waited for: 0 -> 0; matrix products, arithmetic and copies ran while one was open for 0% -> 3% of each run, Pallas kernels for 0% -> 0%
where the time goes in v1:
time: 186 us
  Pallas kernels  161 us (87%)
  local copies, waits for them, and re-layouts  22.8 us (12%)
    pallas_call x1, Pallas kernels, stream(): pl.pallas_call(functools.partial(stream_kernel, n_col, units), grid=(unit...  113 us
    pallas_call x1, Pallas kernels, fold(): pl.pallas_call(functools.partial(fold_kernel, n_row, n_col), out_shape=ja...  25.3 us
    pallas_call x1, Pallas kernels, spread(): pl.pallas_call(functools.partial(spread_kernel, n_row, n_col), out_shape=...  22.7 us
    gather x2, local copies, waits for them, and re-layouts, on_device(): taken = jnp.take(skies, jnp.clip(local_idx, 0, rows_blk - 1), axis=0)  9.38 us
    unnamed x4, local copies, waits for them, and re-layouts  7.22 us
    reshape x1, local copies, waits for them, and re-layouts, on_device(): return (out.transpose(0, 2, 1).reshape(rows_blk, sims), projection.T)  6.17 us
  transfers between devices with their start and end apart: 1, of which 0 were waited for; matrix products, arithmetic and copies ran while one was open for 3% of the time, Pallas kernels for 0%

profile of v1, /device:TPU:0, one launch (start us, length us, event | category | flops | bytes accessed | tf_op | source)
XLA Modules:
  0.0 186.1 jit_solution(15531698549302885383)
XLA Ops:
  0.6 0.7 compare_and_fusion.1
  1.3 0.7 fusion
  2.1 0.0 copy-start
  2.1 6.6 %copy.10 = bf16[24576,64]{1,0:T(8,128)(2,1)} copy(bf16[24576,64]{0,1:T(8,128)(2,1)} %param.7) | data formatting | bytes 6291456 | tf_op args[1]
  8.6 9.2 %gather_fusion = bf16[2048,64]{1,0:T(8,128)(2,1)S(1)} fusion(bf16[24576,64]{1,0:T(8,128)(2,1)} %copy.10, s32[2048]{0:T(1024)S(1)} %fusion), kind=kCustom, calls=%fused_computation | custom fusion | bytes 532480 | tf_op jit(solution)/shard_map/jit(_take)/gather | solution.py:373
  17.8 0.2 copy.11
  18.1 22.7 %spread.1.p_ref = bf16[256,512]{1,0:T(8,128)(2,1)S(1)} custom-call(bf16[64,2048]{1,0:T(8,128)(2,1)S(1)} %select_bitcast_fusion.own_ref), custom_call_target="tpu_custom_call" | custom-call | tf_op jit(solution)/shard_map/spread/pallas_call | solution.py:92
  40.8 0.0 copy-done
  40.8 112.8 %stream.1 = (f32[4,64,6144]{2,1,0:T(8,128)}, f32[2,64,2048]{2,1,0:T(8,128)S(1)}, f32[2,64,2048]{2,1,0:T(8,128)S(1)}) custom-call(bf16[256,512]{1,0:T(8,128)(2,1)S(1)} %spread.1.p_ref, bf16[4,6144,512]{2,1,0:T(8,128)(2,1)} %bitcast.13, f32[64,24576]{1,0:T(8,128)} %bitcast.9, f32[64,24576]{1,0:T(8,128)} %bitcast.10, f32[64,24576]{1,0:T(8,128)} %bitcast.11, ...), custom_call_target="tpu_custom_call" | custom-call | tf_op jit(solution)/shard_map/stream/pallas_call | solution.py:335
  153.6 0.3 collective-permute-start
  153.9 6.2 %copy.13 = f32[4,8,8,6144]{3,2,0,1:T(8,128)} copy(f32[4,8,8,6144]{3,2,1,0:T(8,128)} %bitcast.15) | data formatting | bytes 12582912 | tf_op jit(solution)/shard_map/reshape | solution.py:380
  160.1 0.0 collective-permute-done.swapped_ref
  160.1 25.3 %fold.1 = f32[64,256]{1,0:T(8,128)S(1)} custom-call(f32[2,64,2048]{2,1,0:T(8,128)S(1)} %get-tuple-element.6.acc_ref, f32[2,64,2048]{2,1,0:T(8,128)S(1)} %collective-permute-done.swapped_ref), custom_call_target="tpu_custom_call" | custom-call | tf_op jit(solution)/shard_map/fold/pallas_call | solution.py:192
  185.4 0.6 copy.15
  (2 shorter events, 0.1 us)
Async XLA Ops:
  2.1 38.7 %copy-start = (f32[24576]{0:T(1024)S(1)}, f32[24576]{0:T(1024)}, u32[]{:S(2)}) copy-start(f32[24576]{0:T(1024)} %param.10) | copy-start | bytes 294916
  153.6 6.5 %collective-permute-start = (f32[2,64,2048]{2,1,0:T(8,128)S(1)}, f32[2,64,2048]{2,1,0:T(8,128)S(1)}, u32[]{:S(2)}, u32[]{:S(2)}) collective-permute-start(f32[2,64,2048]{2,1,0:T(8,128)S(1)} %get-tuple-element.7), channel_id=1, source_target_pairs={{0,1},{1,0},{2,3},{3,2},{4,5},{5,4},{6,7},{7,6},{8,9},{9,8},{10,11... | collective-permute-start | bytes 3145736 | tf_op jit(solution)/shard_map/ppermute | solution.py:378

commit v2 on v1

--- a/solution.py
+++ b/solution.py
@@ -21,8 +21,30 @@
     )
 
 
+def meet(devices):
+    barrier = pltpu.get_barrier_semaphore()
+    for device in devices:
+        pl.semaphore_signal(barrier, inc=1, device_id=device, device_id_type=MESH)
+    pl.semaphore_wait(barrier, len(devices))
+
+
+def meet_all(n_row, n_col):
+    barrier = pltpu.get_barrier_semaphore()
+    me = lax.axis_index("row") * n_col + lax.axis_index("col")
+    every = n_row * n_col
+
+    def tell(i, carry):
+        to = lax.rem(me + i, every)
+        pl.semaphore_signal(barrier, inc=1, device_id=(lax.div(to, n_col), lax.rem(to, n_col)), device_id_type=MESH)
+        return carry
+
+    lax.fori_loop(1, every, tell, 0)
+    pl.semaphore_wait(barrier, every - 1)
+
+
 def spread_kernel(n_row, n_col, own_ref, out_ref, land, mine, gather, send1, recv1, send2, recv2):
     r, c = lax.axis_index("row"), lax.axis_index("col")
+    meet_all(n_row, n_col)
     sims, panel = own_ref.shape
     part = panel // n_row
     rep = n_row // n_col
@@ -103,7 +125,7 @@
             pltpu.SemaphoreType.DMA((n_row,)),
             pltpu.SemaphoreType.DMA((n_row,)),
         ],
-        compiler_params=pltpu.CompilerParams(has_side_effects=True, vmem_limit_bytes=LIMIT),
+        compiler_params=pltpu.CompilerParams(has_side_effects=True, collective_id=0, vmem_limit_bytes=LIMIT),
         name="spread",
     )(own)
 
@@ -115,6 +137,8 @@
     core, chip = lax.rem(c, 2), lax.div(c, 2)
     low, high = lax.rem(r, 2), lax.div(r, 2)
     beside = high * 2 + 1 - low
+    meet([(r, lax.rem(chip + s, chips) * 2 + core) for s in range(1, chips)]
+         + [(beside, c)] + [(lax.rem(high + d, pairs) * 2 + low, c) for d in range(1, pairs)])
     sims, pb = out_ref.shape
     hs, half = sims // 2, pairs * pb
 
@@ -200,7 +224,7 @@
             dma((chips - 1,)), dma((chips - 1,)), dma((2,)), dma((2,)),
             dma((chips - 1,)), dma((chips - 1,)), dma((2, pairs - 1)), dma((2, pairs - 1)),
         ],
-        compiler_params=pltpu.CompilerParams(has_side_effects=True, vmem_limit_bytes=LIMIT),
+        compiler_params=pltpu.CompilerParams(has_side_effects=True, collective_id=1, vmem_limit_bytes=LIMIT),
         name="fold",
     )(acc, swapped)
 
@@ -231,6 +255,7 @@
 
     @pl.when(g == 0)
     def _():
+        meet([(r, lax.rem(c + d, n_col)) for d in range(1, n_col)])
         for acc in accs:
             acc[...] = jnp.zeros_like(acc)
 
@@ -361,7 +386,7 @@
             dma((2,)), dma((n_near,)), dma((2, chips - 1)), dma((n_far, chips - 1)),
             dma((n_ws, n_col - 1)), dma((n_got, n_col - 1)),
         ],
-        compiler_params=pltpu.CompilerParams(has_side_effects=True, vmem_limit_bytes=LIMIT, dimension_semantics=("arbitrary",)),
+        compiler_params=pltpu.CompilerParams(has_side_effects=True, collective_id=2, vmem_limit_bytes=LIMIT, dimension_semantics=("arbitrary",)),
         name="stream",
     )(picked, obs.reshape(n_col, slab, depth), *[prior] * n_col, apod.reshape(n_col, slab), proj)
 

time: 186 us -> 177 us (0.952)
  Pallas kernels: 161 us -> 151 us
    pallas_call x1, Pallas kernels: 25.3 us -> 21.5 us  [fold(): pl.pallas_call(functools.partial(fold_kernel, n_row, n_col), out_shape=ja...]
    pallas_call x1, Pallas kernels: 22.7 us -> 19.3 us  [spread(): pl.pallas_call(functools.partial(spread_kernel, n_row, n_col), out_shape=...]
    pallas_call x1, Pallas kernels: 113 us -> 111 us  [stream(): pl.pallas_call(functools.partial(stream_kernel, n_col, units), grid=(unit...]
where the time goes in v2:
time: 177 us
  Pallas kernels  151 us (85%)
  local copies, waits for them, and re-layouts  22.8 us (13%)
    pallas_call x1, Pallas kernels, stream(): pl.pallas_call(functools.partial(stream_kernel, n_col, units), grid=(unit...  111 us
    pallas_call x1, Pallas kernels, fold(): pl.pallas_call(functools.partial(fold_kernel, n_row, n_col), out_shape=ja...  21.5 us
    pallas_call x1, Pallas kernels, spread(): pl.pallas_call(functools.partial(spread_kernel, n_row, n_col), out_shape=...  19.3 us
    gather x2, local copies, waits for them, and re-layouts, on_device(): taken = jnp.take(skies, jnp.clip(local_idx, 0, rows_blk - 1), axis=0)  9.38 us
    unnamed x4, local copies, waits for them, and re-layouts  7.22 us
    reshape x1, local copies, waits for them, and re-layouts, on_device(): return (out.transpose(0, 2, 1).reshape(rows_blk, sims), projection.T)  6.17 us
  transfers between devices with their start and end apart: 1, of which 0 were waited for; matrix products, arithmetic and copies ran while one was open for 3% of the time, Pallas kernels for 0%

profile of v2, /device:TPU:0, one launch (start us, length us, event | category | flops | bytes accessed | tf_op | source)
XLA Modules:
  0.0 176.7 jit_solution(12890829769469435124)
XLA Ops:
  0.6 0.7 compare_and_fusion.1
  1.3 0.7 fusion
  2.1 0.0 copy-start
  2.1 6.6 %copy.10 = bf16[24576,64]{1,0:T(8,128)(2,1)} copy(bf16[24576,64]{0,1:T(8,128)(2,1)} %param.7) | data formatting | bytes 6291456 | tf_op args[1]
  8.6 9.2 %gather_fusion = bf16[2048,64]{1,0:T(8,128)(2,1)S(1)} fusion(bf16[24576,64]{1,0:T(8,128)(2,1)} %copy.10, s32[2048]{0:T(1024)S(1)} %fusion), kind=kCustom, calls=%fused_computation | custom fusion | bytes 532480 | tf_op jit(solution)/shard_map/jit(_take)/gather | solution.py:398
  17.8 0.2 copy.11
  18.1 19.3 %spread.1.p_ref = bf16[256,512]{1,0:T(8,128)(2,1)S(1)} custom-call(bf16[64,2048]{1,0:T(8,128)(2,1)S(1)} %select_bitcast_fusion.own_ref), custom_call_target="tpu_custom_call" | custom-call | tf_op jit(solution)/shard_map/spread/pallas_call | solution.py:114
  37.4 0.0 copy-done
  37.4 110.7 %stream.1 = (f32[4,64,6144]{2,1,0:T(8,128)}, f32[2,64,2048]{2,1,0:T(8,128)S(1)}, f32[2,64,2048]{2,1,0:T(8,128)S(1)}) custom-call(bf16[256,512]{1,0:T(8,128)(2,1)S(1)} %spread.1.p_ref, bf16[4,6144,512]{2,1,0:T(8,128)(2,1)} %bitcast.13, f32[64,24576]{1,0:T(8,128)} %bitcast.9, f32[64,24576]{1,0:T(8,128)} %bitcast.10, f32[64,24576]{1,0:T(8,128)} %bitcast.11, ...), custom_call_target="tpu_custom_call" | custom-call | tf_op jit(solution)/shard_map/stream/pallas_call | solution.py:360
  148.1 0.2 collective-permute-start
  148.3 6.2 %copy.13 = f32[4,8,8,6144]{3,2,0,1:T(8,128)} copy(f32[4,8,8,6144]{3,2,1,0:T(8,128)} %bitcast.15) | data formatting | bytes 12582912 | tf_op jit(solution)/shard_map/reshape | solution.py:405
  154.5 0.0 collective-permute-done.swapped_ref
  154.5 21.5 %fold.1 = f32[64,256]{1,0:T(8,128)S(1)} custom-call(f32[2,64,2048]{2,1,0:T(8,128)S(1)} %get-tuple-element.6.acc_ref, f32[2,64,2048]{2,1,0:T(8,128)S(1)} %collective-permute-done.swapped_ref), custom_call_target="tpu_custom_call" | custom-call | tf_op jit(solution)/shard_map/fold/pallas_call | solution.py:216
  176.0 0.6 copy.15
  (2 shorter events, 0.1 us)
Async XLA Ops:
  2.1 35.3 %copy-start = (f32[24576]{0:T(1024)S(1)}, f32[24576]{0:T(1024)}, u32[]{:S(2)}) copy-start(f32[24576]{0:T(1024)} %param.10) | copy-start | bytes 294916
  148.1 6.4 %collective-permute-start = (f32[2,64,2048]{2,1,0:T(8,128)S(1)}, f32[2,64,2048]{2,1,0:T(8,128)S(1)}, u32[]{:S(2)}, u32[]{:S(2)}) collective-permute-start(f32[2,64,2048]{2,1,0:T(8,128)S(1)} %get-tuple-element.7), channel_id=1, source_target_pairs={{0,1},{1,0},{2,3},{3,2},{4,5},{5,4},{6,7},{7,6},{8,9},{9,8},{10,11... | collective-permute-start | bytes 3145736 | tf_op jit(solution)/shard_map/ppermute | solution.py:403
